TPU v7x, 32 devices: a whole 2x2x4 slice. The times are simulated.
32 devices in a mesh: mem: 4 (over z), tile: 8 (over y, x, core).
Axes of the slice: x: 2, y: 2, z: 4, core: 2. Of those that a mesh axis runs over, the one named last changes fastest.
Arguments:
- state: float32 [20, 8, 12960], P('mem', 'tile'), may hold values from -6 to 6
- obs_index: int32 [8, 256], P('tile'), may hold values from 0 to 12959
- obs_count: int32 [8], P('tile'), may hold values from 32 to 256, as said below
- obs_value: float32 [8, 256], P('tile'), may hold values from -8 to 8
- obs_rinv: float32 [8, 256], P('tile'), may hold values from 0.1 to 1
- radius: int32 [8], P('tile'), may hold values from 1 to 2
Outputs:
- analysis: float32 [20, 8, 12960], P('mem', 'tile')
Inputs may be any that keep to these rules, and one draw needn't show every extreme that they name: `obs_count`: at most 256; some tile has exactly 256 in every draw.
All inputs are finite; a program needn't handle non-finite values.
Results may differ from a plain program's by a relative error of at most 0.0003.
Values sent between devices are 32-bit elements; how exact they have to be, the bound alone decides.
A program may use at most 64 MiB of HBM per device.

v0:
```python
import jax
import jax.numpy as jnp
from jax import lax
from jax.sharding import PartitionSpec as P

COLS = 45
BLOCK = 9
HALO = 2
NS_ITERS = 4
highest = lax.Precision.HIGHEST


def shifted(block, axis, distance):
    devices = range(lax.axis_size(axis))
    route = [((i - distance) % len(devices), i) for i in devices]
    return lax.ppermute(block, axis, route)


def block_points(band_id, tile_id, rows_dev):
    half_block = (BLOCK - 1) // 2
    row_blocks = rows_dev // BLOCK
    col_blocks = COLS // BLOCK
    row_ids = band_id * rows_dev + BLOCK * jnp.arange(row_blocks, dtype=jnp.int32) + half_block
    col_ids = tile_id * COLS + BLOCK * jnp.arange(col_blocks, dtype=jnp.int32) + half_block
    point_rows = (
        jnp.broadcast_to(row_ids[:, None], (row_blocks, col_blocks)).reshape(-1).astype(jnp.float32)
    )
    point_cols = (
        jnp.broadcast_to(col_ids[None, :], (row_blocks, col_blocks)).reshape(-1).astype(jnp.float32)
    )
    return (point_rows, point_cols)


def locality(obs_meta, point_rows, point_cols, extent, circle):
    row_gap = jnp.abs(obs_meta[2][None, :] - point_rows[:, None])
    col_gap = jnp.abs(obs_meta[3][None, :] - point_cols[:, None])
    col_gap = jnp.minimum(col_gap, circle - col_gap)
    taper = jnp.maximum(0.0, 1.0 - row_gap / extent) * jnp.maximum(0.0, 1.0 - col_gap / extent)
    return taper * obs_meta[1][None, :]


def add_block(totals, ens_blk, meta_blk, point_rows, point_cols, extent, circle):
    gram_sum, rhs_sum = totals
    centre = jnp.mean(ens_blk, axis=0)
    spread_obs = ens_blk - centre[None, :]
    innovation = meta_blk[0] - centre
    weights = locality(meta_blk, point_rows, point_cols, extent, circle)
    weighted = weights[:, None, :] * spread_obs[None, :, :]
    gram_sum = gram_sum + jnp.einsum("pkj,lj->pkl", weighted, spread_obs, precision=highest)
    rhs_sum = rhs_sum + jnp.einsum("pkj,j->pk", weighted, innovation, precision=highest)
    return (gram_sum, rhs_sum)


def transform(gram_sum, rhs_sum, members):
    identity = jnp.eye(members, dtype=jnp.float32)
    gram_full = gram_sum + (members - 1.0) * identity[None]
    frob_norm = jnp.sqrt(jnp.sum(gram_full * gram_full, axis=(1, 2)))
    iterate = gram_full / frob_norm[:, None, None]
    inv_root = jnp.broadcast_to(identity, gram_full.shape)
    for sweep in range(NS_ITERS):
        middle = 1.5 * identity[None] - 0.5 * jnp.einsum(
            "pij,pjk->pik", inv_root, iterate, precision=highest
        )
        iterate = jnp.einsum("pij,pjk->pik", iterate, middle, precision=highest)
        inv_root = jnp.einsum("pij,pjk->pik", middle, inv_root, precision=highest)
    inv_root = inv_root / jnp.sqrt(frob_norm)[:, None, None]
    inner = jnp.einsum("pij,pj->pi", inv_root, rhs_sum, precision=highest)
    mean_shift = jnp.einsum("pij,pj->pi", inv_root, inner, precision=highest)
    return jnp.sqrt(members - 1.0) * inv_root + mean_shift[:, :, None]


def apply_mix(band_state, mixing, rows_dev):
    members = band_state.shape[0]
    row_blocks = rows_dev // BLOCK
    col_blocks = COLS // BLOCK
    cell_grid = band_state.reshape(members, row_blocks, BLOCK, col_blocks, BLOCK)
    centre = jnp.mean(cell_grid, axis=0)
    spread_state = cell_grid - centre[None]
    mix_blocks = mixing.reshape(row_blocks, col_blocks, members, members)
    result = (
        jnp.einsum("ablk,laibj->kaibj", mix_blocks, spread_state, precision=highest) + centre[None]
    )
    return result.reshape(members, rows_dev * COLS)


def shards(state, obs_index, obs_count, obs_value, obs_rinv, radius):
    groups = lax.axis_size("mem")
    tile_count = lax.axis_size("tile")
    mem_dev = state.shape[0]
    cell_count = state.shape[2]
    members = mem_dev * groups
    band_cells = cell_count // groups
    rows_dev = band_cells // COLS
    circle = 1.0 * COLS * tile_count
    tile_id = lax.axis_index("tile")
    band_id = lax.axis_index("mem")
    slot_count = obs_index.shape[1]
    own_state = state[:, 0, :]
    cell_index = obs_index[0]
    own_obs = jnp.take(own_state, cell_index, axis=1)
    slot_ids = jnp.arange(slot_count, dtype=jnp.int32)
    rinv_live = jnp.where(slot_ids < obs_count[0], obs_rinv[0], 0.0)
    obs_row = (cell_index // COLS).astype(jnp.float32)
    obs_col = (cell_index % COLS + tile_id * COLS).astype(jnp.float32)
    obs_meta = jnp.stack([obs_value[0], rinv_live, obs_row, obs_col])
    offsets = [distance * direction for distance in range(1, HALO + 1) for direction in (1, -1)]
    ensemble = lax.all_gather(own_obs, "mem", axis=0, tiled=True)
    local_rows = jnp.concatenate([ensemble, obs_meta], axis=0)
    pieces = [local_rows]
    for offset in offsets:
        pieces.append(shifted(local_rows, "tile", offset))
    window = jnp.concatenate(pieces, axis=1)
    ens_win = window[:members]
    meta_win = window[members:]
    spread = state.reshape(mem_dev, groups, band_cells)
    gathered_state = lax.all_to_all(spread, "mem", split_axis=1, concat_axis=0, tiled=True)
    point_rows, point_cols = block_points(band_id, tile_id, rows_dev)
    extent = (radius[0] * COLS).astype(jnp.float32)
    points = point_rows.shape[0]
    stride = min(128, slot_count)
    per_piece = slot_count // stride
    segments = len(pieces)
    totals = (
        jnp.zeros((points, members, members), jnp.float32),
        jnp.zeros((points, members), jnp.float32),
    )

    def visit(block_id, carried):
        first_col = block_id * stride
        ens_blk = lax.dynamic_slice_in_dim(ens_win, first_col, stride, 1)
        meta_blk = lax.dynamic_slice_in_dim(meta_win, first_col, stride, 1)
        return add_block(carried, ens_blk, meta_blk, point_rows, point_cols, extent, circle)

    for segment in range(segments):
        weights_row = meta_win[1, segment * slot_count : (segment + 1) * slot_count]
        filled = jnp.sum((weights_row > 0.0).astype(jnp.int32))
        opening = segment * per_piece
        totals = lax.fori_loop(opening, opening + (filled + stride - 1) // stride, visit, totals)
    mixing = transform(totals[0], totals[1], members)
    analysis = apply_mix(gathered_state[:, 0, :], mixing, rows_dev)
    returned = lax.all_to_all(analysis[:, None, :], "mem", split_axis=0, concat_axis=1, tiled=True)
    return returned.reshape(mem_dev, 1, cell_count)


def solution(mesh):
    in_specs = (
        P("mem", "tile", None),
        P("tile", None),
        P("tile"),
        P("tile", None),
        P("tile", None),
        P("tile"),
    )
    out_specs = P("mem", "tile", None)
    return jax.shard_map(shards, mesh=mesh, in_specs=in_specs, out_specs=out_specs, check_vma=False)
```

profile of v0, /device:TPU:5, one launch (start us, length us, event | category | flops | bytes accessed | tf_op | source)
XLA Modules:
  0.0 104.6 jit_solution(1941645143184801129)
XLA Ops:
  0.7 5.1 %copy.32 = f32[5,1,12960]{0,2,1:T(8,128)} copy(f32[5,1,12960]{2,1,0:T(1,128)} %param.16) | data formatting | bytes 518400 | tf_op args[0]
  5.8 3.6 %gather_fusion = f32[256,5]{1,0:T(8,128)S(1)} fusion(f32[5,12960]{0,1:T(8,128)} %bitcast.212, s32[1024]{0:T(1024)S(1)} %pad_clamp_fusion), kind=kCustom, calls=%fused_computation | custom fusion | bytes 11264 | tf_op jit(solution)/shard_map/jit(_take)/gather | solution.py:100
  9.6 10.8 %all-gather = f32[4,5,256]{2,1,0:T(8,128)S(1)} all-gather(f32[1,5,256]{2,1,0:T(8,128)S(1)} %copy.33), channel_id=1, replica_groups=mesh['mem'=4,'tile'=8] {'mem'}, dimensions={0}, use_global_device_ids=true | all-gather | bytes 25600 | tf_op jit(solution)/shard_map/all_gather | solution.py:107
  21.1 1.2 %collective-permute-start.3 = (f32[24,256]{1,0:T(8,128)S(1)}, f32[24,256]{1,0:T(8,128)S(1)}, u32[]{:S(2)}, u32[]{:S(2)}) collective-permute-start(f32[24,256]{1,0:T(8,128)S(1)} %concatenate.6), channel_id=1, source_target_pairs={{2,0},{3,1},{4,2},{5,3},{6,4},{7,5},{0,6},{1,7},{10,8},{11,9},{12,... | collective-permute-start | bytes 73736 | tf_op jit(solution)/shard_map/ppermute | solution.py:16
  22.7 3.8 %collective-permute-start.1 = (f32[24,256]{1,0:T(8,128)S(1)}, f32[24,256]{1,0:T(8,128)S(1)}, u32[]{:S(2)}, u32[]{:S(2)}) collective-permute-start(f32[24,256]{1,0:T(8,128)S(1)} %concatenate.6), channel_id=1, source_target_pairs={{1,0},{2,1},{3,2},{4,3},{5,4},{6,5},{7,6},{0,7},{9,8},{10,9},{11,1... | collective-permute-start | bytes 73736 | tf_op jit(solution)/shard_map/ppermute | solution.py:16
  26.5 2.0 %collective-permute-start = (f32[24,256]{1,0:T(8,128)S(1)}, f32[24,256]{1,0:T(8,128)S(1)}, u32[]{:S(2)}, u32[]{:S(2)}) collective-permute-start(f32[24,256]{1,0:T(8,128)S(1)} %concatenate.6), channel_id=1, source_target_pairs={{7,0},{0,1},{1,2},{2,3},{3,4},{4,5},{5,6},{6,7},{15,8},{8,9},{9,10... | collective-permute-start | bytes 73736 | tf_op jit(solution)/shard_map/ppermute | solution.py:16
  30.2 4.3 %all-to-all-start = ((f32[5,4,3240]{2,0,1:T(8,128)}), f32[5,4,3240]{2,0,1:T(8,128)S(1)}, u32[]{:S(2)}, u32[]{:S(2)}) async-start(f32[5,4,3240]{2,0,1:T(8,128)} %copy.29), calls=%async_computation | async-start | bytes 851968 | tf_op jit(solution)/shard_map/all_to_all | solution.py:116
  41.6 2.6 %while.65 = (s32[]{:T(128)}, f32[40,20,20]{0,2,1:T(8,128)S(1)}, f32[40,20]{0,1:T(8,128)S(1)}, s32[]{:T(128)}, f32[4,1280]{1,0:T(4,128)S(1)}, /*index=5*/f32[]{:T...) while((s32[]{:T(128)}, f32[40,20,20]{0,2,1:T(8,128)S(1)}, ...), condition=%wide.region_4.5_spmd.clone, body=%wide.region_2.4_spmd.clone.sunk | while | flops 26103460 | bytes 275183 | solution.py:138
  42.7 1.5 %convolution_add_fusion.10 = f32[40,20,20]{0,2,1:T(8,128)S(1)} fusion(f32[40,20,20]{0,2,1:T(8,128)S(1)} %get-tuple-element.817, f32[20,128]{1,0:T(8,128)S(1)} %dynamic-slice_subtract_fusion.10, f32[40,128]{1,0:T(8,128)S(1)} %fusion.183), kind=kOutput, calls=%fused_computation.11.clone.1 | convolution fusion | flops 24694400 | bytes 158720 | tf_op jit(solution)/shard_map/while/body/pkj,lj->pkl/dot_general | solution.py:49
  44.2 2.6 %while.66 = (s32[]{:T(128)}, f32[40,20,20]{0,2,1:T(8,128)S(1)}, f32[40,20]{0,1:T(8,128)S(1)}, s32[]{:T(128)}, f32[4,1280]{1,0:T(4,128)S(1)}, /*index=5*/f32[]{:T...) while((s32[]{:T(128)}, f32[40,20,20]{0,2,1:T(8,128)S(1)}, ...), condition=%wide.region_8.9_spmd.clone, body=%wide.region_6.8_spmd.clone.sunk | while | flops 26103460 | bytes 275183 | solution.py:138
  45.3 1.5 %convolution_add_fusion.11 = f32[40,20,20]{0,2,1:T(8,128)S(1)} fusion(f32[40,20,20]{0,2,1:T(8,128)S(1)} %get-tuple-element.856, f32[20,128]{1,0:T(8,128)S(1)} %dynamic-slice_subtract_fusion.11, f32[40,128]{1,0:T(8,128)S(1)} %fusion.189), kind=kOutput, calls=%fused_computation.37.clone.1 | convolution fusion | flops 24694400 | bytes 158720 | tf_op jit(solution)/shard_map/while/body/pkj,lj->pkl/dot_general | solution.py:49
  46.9 2.6 %while.67 = (s32[]{:T(128)}, f32[40,20,20]{0,2,1:T(8,128)S(1)}, f32[40,20]{0,1:T(8,128)S(1)}, s32[]{:T(128)}, f32[4,1280]{1,0:T(4,128)S(1)}, /*index=5*/f32[]{:T...) while((s32[]{:T(128)}, f32[40,20,20]{0,2,1:T(8,128)S(1)}, ...), condition=%wide.region_12.13_spmd.clone, body=%wide.region_10.12_spmd.clone.sunk | while | flops 26103460 | bytes 275183 | solution.py:138
  48.0 1.5 %convolution_add_fusion.12 = f32[40,20,20]{0,2,1:T(8,128)S(1)} fusion(f32[40,20,20]{0,2,1:T(8,128)S(1)} %get-tuple-element.895, f32[20,128]{1,0:T(8,128)S(1)} %dynamic-slice_subtract_fusion.12, f32[40,128]{1,0:T(8,128)S(1)} %fusion.195), kind=kOutput, calls=%fused_computation.63.clone.1 | convolution fusion | flops 24694400 | bytes 158720 | tf_op jit(solution)/shard_map/while/body/pkj,lj->pkl/dot_general | solution.py:49
  49.5 5.3 %while.68 = (s32[]{:T(128)}, f32[40,20,20]{0,2,1:T(8,128)S(1)}, f32[40,20]{0,1:T(8,128)S(1)}, s32[]{:T(128)}, f32[4,1280]{1,0:T(4,128)S(1)}, /*index=5*/f32[]{:T...) while((s32[]{:T(128)}, f32[40,20,20]{0,2,1:T(8,128)S(1)}, ...), condition=%wide.region_16.17_spmd.clone, body=%wide.region_14.16_spmd.clone.sunk | while | flops 26103460 | bytes 275183 | solution.py:138
  50.6 1.5 %convolution_add_fusion.13 = f32[40,20,20]{0,2,1:T(8,128)S(1)} fusion(f32[40,20,20]{0,2,1:T(8,128)S(1)} %get-tuple-element.934, f32[20,128]{1,0:T(8,128)S(1)} %dynamic-slice_subtract_fusion.13, f32[40,128]{1,0:T(8,128)S(1)} %fusion.201), kind=kOutput, calls=%fused_computation.89.clone.1 | convolution fusion | flops 24694400 | bytes 158720 | tf_op jit(solution)/shard_map/while/body/pkj,lj->pkl/dot_general | solution.py:49
  53.3 1.5 %convolution_add_fusion.13 = f32[40,20,20]{0,2,1:T(8,128)S(1)} fusion(f32[40,20,20]{0,2,1:T(8,128)S(1)} %get-tuple-element.934, f32[20,128]{1,0:T(8,128)S(1)} %dynamic-slice_subtract_fusion.13, f32[40,128]{1,0:T(8,128)S(1)} %fusion.201), kind=kOutput, calls=%fused_computation.89.clone.1 | convolution fusion | flops 24694400 | bytes 158720 | tf_op jit(solution)/shard_map/while/body/pkj,lj->pkl/dot_general | solution.py:49
  54.8 2.8 %while.69 = (s32[]{:T(128)}, f32[40,20,20]{0,2,1:T(8,128)S(1)}, f32[40,20]{0,1:T(8,128)S(1)}, s32[]{:T(128)}, f32[4,1280]{1,0:T(4,128)S(1)}, /*index=5*/f32[]{:T...) while((s32[]{:T(128)}, f32[40,20,20]{0,2,1:T(8,128)S(1)}, ...), condition=%wide.region_20.21_spmd.clone, body=%wide.region_18.20_spmd.clone.sunk | while | flops 26103460 | bytes 275183 | solution.py:138
  55.9 1.5 %convolution_add_fusion.14 = f32[40,20,20]{0,2,1:T(8,128)S(1)} fusion(f32[40,20,20]{0,2,1:T(8,128)S(1)} %get-tuple-element.973, f32[20,128]{1,0:T(8,128)S(1)} %dynamic-slice_subtract_fusion.14, f32[40,128]{1,0:T(8,128)S(1)} %fusion.207), kind=kOutput, calls=%fused_computation.115.clone.1 | convolution fusion | flops 24694400 | bytes 158720 | tf_op jit(solution)/shard_map/while/body/pkj,lj->pkl/dot_general | solution.py:49
  72.0 3.7 %reshape_squeeze.3 = f32[20,8,9,5,9]{4,3,2,1,0:T(8,128)} reshape(f32[4,5,1,3240]{3,1,0,2:T(8,128)S(1)} %bitcast.213) | data formatting | bytes 518400 | tf_op jit(solution)/shard_map/reshape;squeeze | solution.py:76
  75.7 4.9 %copy.31 = f32[20,8,9,5,9]{0,4,2,3,1:T(8,128)S(1)} copy(f32[20,8,9,5,9]{4,3,2,1,0:T(8,128)} %reshape_squeeze.3) | data formatting | bytes 518400 | tf_op jit(solution)/shard_map/reshape;squeeze | solution.py:76
  82.0 4.5 %bitcast_add_fusion.5 = f32[20,8,9,5,9]{0,4,2,3,1:T(8,128)S(1)} fusion(f32[8,5,20,20,1]{3,2,4,1,0:T(8,128)} %bitcast.215, f32[20,8,9,5,9]{0,4,2,3,1:T(8,128)S(1)} %copy.31, f32[8,9,5,9]{3,1,2,0:T(8,128)S(1)} %copy.30), kind=kOutput, calls=%fused_computation.141 | convolution fusion | flops 15681600 | bytes 595360 | tf_op jit(solution)/shard_map/ablk,laibj->kaibj/dot_general | solution.py:81
  86.7 1.4 %broadcast_in_dim_reshape.3 = f32[20,1,3240]{0,2,1:T(8,128)} reshape(f32[20,8,9,5,9]{0,4,3,2,1:T(8,128)S(1)} %copy.36) | data formatting | bytes 518400 | tf_op jit(solution)/shard_map/broadcast_in_dim;reshape | solution.py:141
  88.1 1.8 %copy.37 = f32[20,1,3240]{2,1,0:T(1,128)S(1)} copy(f32[20,1,3240]{0,2,1:T(8,128)} %broadcast_in_dim_reshape.3) | data formatting | bytes 518400 | tf_op jit(solution)/shard_map/broadcast_in_dim;reshape | solution.py:141
  89.9 13.5 %all_to_all.30 = f32[20,1,3240]{2,1,0:T(1,128)S(1)} all-to-all(f32[20,1,3240]{2,1,0:T(1,128)S(1)} %copy.37), channel_id=1, replica_groups=mesh['mem'=4,'tile'=8] {'mem'}, dimensions={0} | all-to-all | bytes 518400 | tf_op jit(solution)/shard_map/all_to_all | solution.py:141
  (148 shorter events, 29.3 us)
Async XLA Ops:
  0.7 5.1 %copy-start.2 = (s32[1,256]{1,0:T(1,128)S(1)}, s32[1,256]{1,0:T(1,128)}, u32[]{:S(2)}) copy-start(s32[1,256]{1,0:T(1,128)} %param.17) | copy-start | bytes 3076
  0.7 19.7 %copy-start.3 = (f32[1,256]{1,0:T(1,128)S(1)}, f32[1,256]{1,0:T(1,128)}, u32[]{:S(2)}) copy-start(f32[1,256]{1,0:T(1,128)} %param.20) | copy-start | bytes 3076
  0.7 20.4 %copy-start.4 = (f32[1,256]{1,0:T(1,128)S(1)}, f32[1,256]{1,0:T(1,128)}, u32[]{:S(2)}) copy-start(f32[1,256]{1,0:T(1,128)} %param.19) | copy-start | bytes 3076
  0.7 27.8 %copy-start.1 = (f32[5,1,12960]{2,1,0:T(1,128)S(1)}, f32[5,1,12960]{2,1,0:T(1,128)}, u32[]{:S(2)}) copy-start(f32[5,1,12960]{2,1,0:T(1,128)} %param.16) | copy-start | bytes 777604
  21.1 14.8 %collective-permute-start.3 = (f32[24,256]{1,0:T(8,128)S(1)}, f32[24,256]{1,0:T(8,128)S(1)}, u32[]{:S(2)}, u32[]{:S(2)}) collective-permute-start(f32[24,256]{1,0:T(8,128)S(1)} %concatenate.6), channel_id=1, source_target_pairs={{2,0},{3,1},{4,2},{5,3},{6,4},{7,5},{0,6},{1,7},{10,8},{11,9},{12,... | collective-permute-start | bytes 73736 | tf_op jit(solution)/shard_map/ppermute | solution.py:16
  22.3 14.3 %collective-permute-start.2 = (f32[24,256]{1,0:T(8,128)S(1)}, f32[24,256]{1,0:T(8,128)S(1)}, u32[]{:S(2)}, u32[]{:S(2)}) collective-permute-start(f32[24,256]{1,0:T(8,128)S(1)} %concatenate.6), channel_id=1, source_target_pairs={{6,0},{7,1},{0,2},{1,3},{2,4},{3,5},{4,6},{5,7},{14,8},{15,9},{8,1... | collective-permute-start | bytes 73736 | tf_op jit(solution)/shard_map/ppermute | solution.py:16
  22.7 14.7 %collective-permute-start.1 = (f32[24,256]{1,0:T(8,128)S(1)}, f32[24,256]{1,0:T(8,128)S(1)}, u32[]{:S(2)}, u32[]{:S(2)}) collective-permute-start(f32[24,256]{1,0:T(8,128)S(1)} %concatenate.6), channel_id=1, source_target_pairs={{1,0},{2,1},{3,2},{4,3},{5,4},{6,5},{7,6},{0,7},{9,8},{10,9},{11,1... | collective-permute-start | bytes 73736 | tf_op jit(solution)/shard_map/ppermute | solution.py:16
  26.5 13.5 %collective-permute-start = (f32[24,256]{1,0:T(8,128)S(1)}, f32[24,256]{1,0:T(8,128)S(1)}, u32[]{:S(2)}, u32[]{:S(2)}) collective-permute-start(f32[24,256]{1,0:T(8,128)S(1)} %concatenate.6), channel_id=1, source_target_pairs={{7,0},{0,1},{1,2},{2,3},{3,4},{4,5},{5,6},{6,7},{15,8},{8,9},{9,10... | collective-permute-start | bytes 73736 | tf_op jit(solution)/shard_map/ppermute | solution.py:16
  30.2 41.1 %all-to-all-start = ((f32[5,4,3240]{2,0,1:T(8,128)}), f32[5,4,3240]{2,0,1:T(8,128)S(1)}, u32[]{:S(2)}, u32[]{:S(2)}) async-start(f32[5,4,3240]{2,0,1:T(8,128)} %copy.29), calls=%async_computation | async-start | bytes 851968 | tf_op jit(solution)/shard_map/all_to_all | solution.py:116
  71.3 0.8 copy-start
where the time goes:
time: 105 us
  matrix products  28.1 us (27%)
  local copies, waits for them, and re-layouts  27.2 us (26%)
  blocking collectives  24.2 us (23%)
  starting transfers between devices  11.7 us (11%)
  other arithmetic  7.44 us (7%)
  between operations  5.13 us (5%)
    all_to_all x1, blocking collectives, shards(): lax.all_to_all(analysis[:, None, :], 'mem', split_axis=0, concat_axis=1,...  13.5 us
    all_gather x1, blocking collectives, shards(): ensemble = lax.all_gather(own_obs, 'mem', axis=0, tiled=True)  10.8 us
    dot_general x6, matrix products, add_block(): jnp.einsum('pkj,lj->pkl', weighted, spread_obs, precision=highest)  8.91 us
    another operation x2, local copies, waits for them, and re-layouts, apply_mix(): band_state.reshape(members, row_blocks, BLOCK, col_blocks, BLOCK)  8.62 us
    ppermute x4, starting transfers between devices, shifted(): return lax.ppermute(block, axis, route)  7.34 us
    unnamed x17, local copies, waits for them, and re-layouts  5.97 us
    dot_general x1, matrix products, apply_mix(): jnp.einsum('ablk,laibj->kaibj', mix_blocks, spread_state, precision=highest)  4.5 us
    all_to_all x1, starting transfers between devices, shards(): lax.all_to_all(spread, 'mem', split_axis=1, concat_axis=0, tiled=True)  4.35 us
  transfers between devices with their start and end apart: 5, of which 0 were waited for; matrix products, arithmetic and copies ran while one was open for 32% of the time, Pallas kernels for 0%

commit v1 on v0

--- a/solution.py
+++ b/solution.py
@@ -138,7 +138,12 @@
         totals = lax.fori_loop(opening, opening + (filled + stride - 1) // stride, visit, totals)
     mixing = transform(totals[0], totals[1], members)
     analysis = apply_mix(gathered_state[:, 0, :], mixing, rows_dev)
-    returned = lax.all_to_all(analysis[:, None, :], "mem", split_axis=0, concat_axis=1, tiled=True)
+    returned = jnp.concatenate(
+        lax.all_to_all(
+            jnp.stack(jnp.split(analysis[:, None, :], lax.axis_size("mem"), axis=0)), "mem", 0, 0
+        ),
+        axis=1,
+    )
     return returned.reshape(mem_dev, 1, cell_count)
 
 

time: 105 us -> 140 us (1.33)
  local copies, waits for them, and re-layouts: 27.2 us -> 62.3 us
    split x0 -> x5, local copies, waits for them, and re-layouts: none -> 30.8 us  [shards(): jnp.split(analysis[:, None, :], lax.axis_size('mem'), axis=0)]
    another operation x2 -> x6, local copies, waits for them, and re-layouts: 3.16 us -> 8.83 us  [the longest x5 7.66 us: shards(): jnp.stack(jnp.split(analysis[:, None, :], lax.axis_size('mem'), axis=0))]
    unnamed x17 -> x15, local copies, waits for them, and re-layouts: 5.97 us -> 5.2 us
  transfers between devices with their start and end apart: 5 -> 5, of which waited for: 0 -> 0; matrix products, arithmetic and copies ran while one was open for 32% -> 23% of each run, Pallas kernels for 0% -> 0%
where the time goes in v1:
time: 140 us; the launch traced here: 139 us
  local copies, waits for them, and re-layouts  62.3 us (44%)
  matrix products  28.2 us (20%)
  blocking collectives  24.2 us (17%)
  starting transfers between devices  11.7 us (8%)
  other arithmetic  6.94 us (5%)
  between operations  5.14 us (4%)
    split x5, local copies, waits for them, and re-layouts, shards(): jnp.split(analysis[:, None, :], lax.axis_size('mem'), axis=0)  30.8 us
    all_to_all x1, blocking collectives, shards(): lax.all_to_all(jnp.stack(jnp.split(analysis[:, None, :], lax.axis_size('m...  13.5 us
    all_gather x1, blocking collectives, shards(): ensemble = lax.all_gather(own_obs, 'mem', axis=0, tiled=True)  10.8 us
    dot_general x6, matrix products, add_block(): jnp.einsum('pkj,lj->pkl', weighted, spread_obs, precision=highest)  8.79 us
    another operation x2, local copies, waits for them, and re-layouts, apply_mix(): band_state.reshape(members, row_blocks, BLOCK, col_blocks, BLOCK)  8.62 us
    another operation x5, local copies, waits for them, and re-layouts, shards(): jnp.stack(jnp.split(analysis[:, None, :], lax.axis_size('mem'), axis=0))  7.66 us
    ppermute x4, starting transfers between devices, shifted(): return lax.ppermute(block, axis, route)  7.34 us
    unnamed x15, local copies, waits for them, and re-layouts  5.2 us
  transfers between devices with their start and end apart: 5, of which 0 were waited for; matrix products, arithmetic and copies ran while one was open for 23% of the time, Pallas kernels for 0%

profile of v1, /device:TPU:5, one launch (start us, length us, event | category | flops | bytes accessed | tf_op | source)
XLA Modules:
  0.0 139.2 jit_solution(3676575363834728565)
XLA Ops:
  2.1 5.1 %copy.36 = f32[5,1,12960]{0,2,1:T(8,128)} copy(f32[5,1,12960]{2,1,0:T(1,128)} %param.16) | data formatting | bytes 518400 | tf_op args[0]
  7.2 3.6 %gather_fusion = f32[256,5]{1,0:T(8,128)S(1)} fusion(f32[5,12960]{0,1:T(8,128)} %bitcast.208, s32[1024]{0:T(1024)S(1)} %pad_clamp_fusion), kind=kCustom, calls=%fused_computation | custom fusion | bytes 11264 | tf_op jit(solution)/shard_map/jit(_take)/gather | solution.py:100
  10.9 10.8 %all-gather = f32[4,5,256]{2,1,0:T(8,128)S(1)} all-gather(f32[1,5,256]{2,1,0:T(8,128)S(1)} %copy.37), channel_id=1, replica_groups=mesh['mem'=4,'tile'=8] {'mem'}, dimensions={0}, use_global_device_ids=true | all-gather | bytes 25600 | tf_op jit(solution)/shard_map/all_gather | solution.py:107
  24.0 3.8 %collective-permute-start.1 = (f32[24,256]{1,0:T(8,128)S(1)}, f32[24,256]{1,0:T(8,128)S(1)}, u32[]{:S(2)}, u32[]{:S(2)}) collective-permute-start(f32[24,256]{1,0:T(8,128)S(1)} %concatenate.6), channel_id=1, source_target_pairs={{1,0},{2,1},{3,2},{4,3},{5,4},{6,5},{7,6},{0,7},{9,8},{10,9},{11,1... | collective-permute-start | bytes 73736 | tf_op jit(solution)/shard_map/ppermute | solution.py:16
  27.8 2.0 %collective-permute-start = (f32[24,256]{1,0:T(8,128)S(1)}, f32[24,256]{1,0:T(8,128)S(1)}, u32[]{:S(2)}, u32[]{:S(2)}) collective-permute-start(f32[24,256]{1,0:T(8,128)S(1)} %concatenate.6), channel_id=1, source_target_pairs={{7,0},{0,1},{1,2},{2,3},{3,4},{4,5},{5,6},{6,7},{15,8},{8,9},{9,10... | collective-permute-start | bytes 73736 | tf_op jit(solution)/shard_map/ppermute | solution.py:16
  31.5 4.3 %all-to-all-start = ((f32[5,4,3240]{2,0,1:T(8,128)}), f32[5,4,3240]{2,0,1:T(8,128)S(1)}, u32[]{:S(2)}, u32[]{:S(2)}) async-start(f32[5,4,3240]{2,0,1:T(8,128)} %copy.33), calls=%async_computation | async-start | bytes 851968 | tf_op jit(solution)/shard_map/all_to_all | solution.py:116
  42.9 2.6 %while.65 = (s32[]{:T(128)}, f32[40,20,20]{0,2,1:T(8,128)S(1)}, f32[40,20]{0,1:T(8,128)S(1)}, s32[]{:T(128)}, f32[4,1280]{1,0:T(4,128)S(1)}, /*index=5*/f32[]{:T...) while((s32[]{:T(128)}, f32[40,20,20]{0,2,1:T(8,128)S(1)}, ...), condition=%wide.region_4.5_spmd.clone, body=%wide.region_2.4_spmd.clone.sunk | while | flops 26103460 | bytes 275183 | solution.py:138
  45.5 2.6 %while.66 = (s32[]{:T(128)}, f32[40,20,20]{0,2,1:T(8,128)S(1)}, f32[40,20]{0,1:T(8,128)S(1)}, s32[]{:T(128)}, f32[4,1280]{1,0:T(4,128)S(1)}, /*index=5*/f32[]{:T...) while((s32[]{:T(128)}, f32[40,20,20]{0,2,1:T(8,128)S(1)}, ...), condition=%wide.region_8.9_spmd.clone, body=%wide.region_6.8_spmd.clone.sunk | while | flops 26103460 | bytes 275183 | solution.py:138
  48.1 2.6 %while.67 = (s32[]{:T(128)}, f32[40,20,20]{0,2,1:T(8,128)S(1)}, f32[40,20]{0,1:T(8,128)S(1)}, s32[]{:T(128)}, f32[4,1280]{1,0:T(4,128)S(1)}, /*index=5*/f32[]{:T...) while((s32[]{:T(128)}, f32[40,20,20]{0,2,1:T(8,128)S(1)}, ...), condition=%wide.region_12.13_spmd.clone, body=%wide.region_10.12_spmd.clone.sunk | while | flops 26103460 | bytes 275183 | solution.py:138
  50.7 5.2 %while.68 = (s32[]{:T(128)}, f32[40,20,20]{0,2,1:T(8,128)S(1)}, f32[40,20]{0,1:T(8,128)S(1)}, s32[]{:T(128)}, f32[4,1280]{1,0:T(4,128)S(1)}, /*index=5*/f32[]{:T...) while((s32[]{:T(128)}, f32[40,20,20]{0,2,1:T(8,128)S(1)}, ...), condition=%wide.region_16.17_spmd.clone, body=%wide.region_14.16_spmd.clone.sunk | while | flops 26103460 | bytes 275183 | solution.py:138
  55.9 2.8 %while.69 = (s32[]{:T(128)}, f32[40,20,20]{0,2,1:T(8,128)S(1)}, f32[40,20]{0,1:T(8,128)S(1)}, s32[]{:T(128)}, f32[4,1280]{1,0:T(4,128)S(1)}, /*index=5*/f32[]{:T...) while((s32[]{:T(128)}, f32[40,20,20]{0,2,1:T(8,128)S(1)}, ...), condition=%wide.region_20.21_spmd.clone, body=%wide.region_18.20_spmd.clone.sunk | while | flops 26103460 | bytes 275183 | solution.py:138
  72.8 3.7 %reshape_squeeze.3 = f32[20,8,9,5,9]{4,3,2,1,0:T(8,128)} reshape(f32[4,5,1,3240]{3,1,0,2:T(8,128)S(1)} %bitcast.209) | data formatting | bytes 518400 | tf_op jit(solution)/shard_map/reshape;squeeze | solution.py:76
  76.5 4.9 %copy.35 = f32[20,8,9,5,9]{0,4,2,3,1:T(8,128)S(1)} copy(f32[20,8,9,5,9]{4,3,2,1,0:T(8,128)} %reshape_squeeze.3) | data formatting | bytes 518400 | tf_op jit(solution)/shard_map/reshape;squeeze | solution.py:76
  81.4 4.6 %bitcast_add_fusion.5 = f32[20,8,9,5,9]{0,4,2,3,1:T(8,128)S(1)} fusion(f32[8,5,20,20,1]{3,2,4,1,0:T(8,128)S(1)} %bitcast.211, f32[20,8,9,5,9]{0,4,2,3,1:T(8,128)S(1)} %copy.35, f32[8,9,5,9]{3,1,2,0:T(8,128)} %copy.34), kind=kOutput, calls=%fused_computation.141 | convolution fusion | flops 15681600 | bytes 595360 | tf_op jit(solution)/shard_map/ablk,laibj->kaibj/dot_general | solution.py:81
  86.0 5.7 %fusion.118 = (f32[5,8,9,5,9]{0,4,2,3,1:T(8,128)}, f32[5,8,9,5,9]{0,4,2,3,1:T(8,128)}, f32[5,8,9,5,9]{0,4,2,3,1:T(8,128)}, f32[5,8,9,5,9]{0,4,2,3,1:T(8,128)S(1)}) fusion(f32[20,8,9,5,9]{0,4,2,3,1:T(8,128)S(1)} %bitcast_add_fusion.5), kind=kLoop, calls=%fused_computation.196 | loop fusion | bytes 518400 | tf_op jit(solution)/shard_map/split | solution.py:143
  91.7 6.6 %copy.40 = f32[5,8,9,5,9]{4,3,2,1,0:T(8,128)} copy(f32[5,8,9,5,9]{0,4,2,3,1:T(8,128)} %get-tuple-element.487) | data formatting | bytes 129600 | tf_op jit(solution)/shard_map/split | solution.py:143
  98.3 1.8 %stack.18 = f32[1,5,1,3240]{3,1,2,0:T(8,128)S(1)} reshape(f32[5,8,9,5,9]{4,3,2,1,0:T(8,128)} %copy.40) | data formatting | bytes 129600 | tf_op jit(solution)/shard_map/stack | solution.py:143
  100.2 6.5 %copy.43 = f32[5,8,9,5,9]{4,3,2,1,0:T(8,128)} copy(f32[5,8,9,5,9]{0,4,2,3,1:T(8,128)} %get-tuple-element.488) | data formatting | bytes 129600 | tf_op jit(solution)/shard_map/split | solution.py:143
  106.7 1.8 %stack.21 = f32[1,5,1,3240]{3,1,2,0:T(8,128)S(1)} reshape(f32[5,8,9,5,9]{4,3,2,1,0:T(8,128)} %copy.43) | data formatting | bytes 129600 | tf_op jit(solution)/shard_map/stack | solution.py:143
  108.5 6.5 %copy.42 = f32[5,8,9,5,9]{4,3,2,1,0:T(8,128)} copy(f32[5,8,9,5,9]{0,4,2,3,1:T(8,128)} %get-tuple-element.489) | data formatting | bytes 129600 | tf_op jit(solution)/shard_map/split | solution.py:143
  115.1 1.8 %stack.20 = f32[1,5,1,3240]{3,1,2,0:T(8,128)S(1)} reshape(f32[5,8,9,5,9]{4,3,2,1,0:T(8,128)} %copy.42) | data formatting | bytes 129600 | tf_op jit(solution)/shard_map/stack | solution.py:143
  116.9 5.4 %copy.41 = f32[5,8,9,5,9]{4,3,2,1,0:T(8,128)} copy(f32[5,8,9,5,9]{0,4,2,3,1:T(8,128)S(1)} %get-tuple-element.490) | data formatting | bytes 129600 | tf_op jit(solution)/shard_map/split | solution.py:143
  122.3 1.8 %stack.19 = f32[1,5,1,3240]{3,1,2,0:T(8,128)S(1)} reshape(f32[5,8,9,5,9]{4,3,2,1,0:T(8,128)} %copy.41) | data formatting | bytes 129600 | tf_op jit(solution)/shard_map/stack | solution.py:143
  124.5 13.5 %all_to_all.20 = f32[4,5,1,3240]{3,2,1,0:T(1,128)S(1)} all-to-all(f32[4,5,1,3240]{3,2,1,0:T(1,128)S(1)} %copy.44), channel_id=1, replica_groups=mesh['mem'=4,'tile'=8] {'mem'}, dimensions={0} | all-to-all | bytes 518400 | tf_op jit(solution)/shard_map/all_to_all | solution.py:142
  (154 shorter events, 38.9 us)
Async XLA Ops:
  2.0 19.7 %copy-start.1 = (s32[1,256]{1,0:T(1,128)S(1)}, s32[1,256]{1,0:T(1,128)}, u32[]{:S(2)}) copy-start(s32[1,256]{1,0:T(1,128)} %param.17) | copy-start | bytes 3076
  2.0 19.7 %copy-start.2 = (f32[1,256]{1,0:T(1,128)S(1)}, f32[1,256]{1,0:T(1,128)}, u32[]{:S(2)}) copy-start(f32[1,256]{1,0:T(1,128)} %param.20) | copy-start | bytes 3076
  2.1 20.4 %copy-start.3 = (f32[1,256]{1,0:T(1,128)S(1)}, f32[1,256]{1,0:T(1,128)}, u32[]{:S(2)}) copy-start(f32[1,256]{1,0:T(1,128)} %param.19) | copy-start | bytes 3076
  2.1 27.8 %copy-start = (f32[5,1,12960]{2,1,0:T(1,128)S(1)}, f32[5,1,12960]{2,1,0:T(1,128)}, u32[]{:S(2)}) copy-start(f32[5,1,12960]{2,1,0:T(1,128)} %param.16) | copy-start | bytes 777604
  22.5 14.8 %collective-permute-start.3 = (f32[24,256]{1,0:T(8,128)S(1)}, f32[24,256]{1,0:T(8,128)S(1)}, u32[]{:S(2)}, u32[]{:S(2)}) collective-permute-start(f32[24,256]{1,0:T(8,128)S(1)} %concatenate.6), channel_id=1, source_target_pairs={{2,0},{3,1},{4,2},{5,3},{6,4},{7,5},{0,6},{1,7},{10,8},{11,9},{12,... | collective-permute-start | bytes 73736 | tf_op jit(solution)/shard_map/ppermute | solution.py:16
  23.7 14.3 %collective-permute-start.2 = (f32[24,256]{1,0:T(8,128)S(1)}, f32[24,256]{1,0:T(8,128)S(1)}, u32[]{:S(2)}, u32[]{:S(2)}) collective-permute-start(f32[24,256]{1,0:T(8,128)S(1)} %concatenate.6), channel_id=1, source_target_pairs={{6,0},{7,1},{0,2},{1,3},{2,4},{3,5},{4,6},{5,7},{14,8},{15,9},{8,1... | collective-permute-start | bytes 73736 | tf_op jit(solution)/shard_map/ppermute | solution.py:16
  24.0 14.6 %collective-permute-start.1 = (f32[24,256]{1,0:T(8,128)S(1)}, f32[24,256]{1,0:T(8,128)S(1)}, u32[]{:S(2)}, u32[]{:S(2)}) collective-permute-start(f32[24,256]{1,0:T(8,128)S(1)} %concatenate.6), channel_id=1, source_target_pairs={{1,0},{2,1},{3,2},{4,3},{5,4},{6,5},{7,6},{0,7},{9,8},{10,9},{11,1... | collective-permute-start | bytes 73736 | tf_op jit(solution)/shard_map/ppermute | solution.py:16
  27.8 13.4 %collective-permute-start = (f32[24,256]{1,0:T(8,128)S(1)}, f32[24,256]{1,0:T(8,128)S(1)}, u32[]{:S(2)}, u32[]{:S(2)}) collective-permute-start(f32[24,256]{1,0:T(8,128)S(1)} %concatenate.6), channel_id=1, source_target_pairs={{7,0},{0,1},{1,2},{2,3},{3,4},{4,5},{5,6},{6,7},{15,8},{8,9},{9,10... | collective-permute-start | bytes 73736 | tf_op jit(solution)/shard_map/ppermute | solution.py:16
  31.5 40.2 %all-to-all-start = ((f32[5,4,3240]{2,0,1:T(8,128)}), f32[5,4,3240]{2,0,1:T(8,128)S(1)}, u32[]{:S(2)}, u32[]{:S(2)}) async-start(f32[5,4,3240]{2,0,1:T(8,128)} %copy.33), calls=%async_computation | async-start | bytes 851968 | tf_op jit(solution)/shard_map/all_to_all | solution.py:116
